TPU v7x, 32 devices: a whole 2x2x4 slice. The times are simulated.
32 devices in a mesh: groups: 2 (over x), band: 16 (over z, y, core).
Axes of the slice: x: 2, y: 2, z: 4, core: 2. Of those that a mesh axis runs over, the one named last changes fastest.
Arguments:
- orbitals: bfloat16 [2560, 32, 128], P(('groups', 'band')), parts along dimension 0, may hold values from -24 to 24
- potential: float32 [64, 128], P('groups'), parts along dimension 0, may hold values from -2 to 0
- plan: int32 [4, 16], P('groups'), parts along dimension 0, may hold values from 0 to 15, as said below
- owners: int32 [4, 16], P('groups'), parts along dimension 0, may hold values from 0 to 15, each once within a row
Outputs:
- filtered: bfloat16 [2560, 32, 128], P(('groups', 'band')), parts along dimension 0
- tiles: float32 [2, 2560, 80], P(None, ('groups', 'band')), parts along dimension 1
There are 2 independent parts, one for each index of `groups`. A program takes and returns all parts, laid end to end along the dimension named above; each array names one. Nothing has to cross between parts.
Inputs may be any that keep to these rules, and one draw needn't show every extreme that they name: In each of the 2 rounds the band groups are paired by a round-robin tournament: plan[r, i] is never i and plan[r, plan[r, i]] = i. `owners`: each row is a permutation of the band groups.
All inputs are finite; a program needn't handle non-finite values.
Results may differ from a plain program's by a relative error of at most 0.0055.
Values may be sent and summed in bfloat16 or wider, within the bound.
A program may use at most 192 MiB of HBM per device.

v0:
```python
import math

import jax
import jax.numpy as jnp
from jax import lax
from jax.sharding import PartitionSpec as P

NZ = 16
ROUNDS = 2


lower_edge = -2.5
cutoff_edge = 4.0
upper_edge = 8.5
half_width = (upper_edge - cutoff_edge) / 2.0
middle_point = (upper_edge + cutoff_edge) / 2.0


def with_halo(array, sides, width):
    for axis, dim in sides:
        devices, length = (lax.axis_size(axis), array.shape[dim])
        up = [(i, (i + 1) % devices) for i in range(devices - 1)]
        down = [(j, i) for i, j in up]
        last = lax.slice_in_dim(array, length - width, length, axis=dim)
        leading = lax.slice_in_dim(array, 0, width, axis=dim)
        before = lax.ppermute(last, axis, up)
        after = lax.ppermute(leading, axis, down)
        array = jnp.concatenate([before, array, after], axis=dim)
    return array


def chebyshev_filter(start_values, operator):
    sigma_zero = half_width / (lower_edge - middle_point)
    previous = start_values
    current = sigma_zero / half_width * (operator(start_values) - middle_point * start_values)
    sigma_now = sigma_zero
    sigma_next = 1.0 / (2.0 / sigma_zero - sigma_now)
    following = (
        2.0 * sigma_next / half_width * (operator(current) - middle_point * current)
        - sigma_now * sigma_next * previous
    )
    previous, current, sigma_now = (current, following, sigma_next)
    return current


def plane_part(center):
    span = center.shape[-1]
    margin = 2 * NZ
    padded = jnp.pad(center, ((0, 0), (0, 0), (margin, margin)))
    z_pos = jnp.arange(span, dtype=jnp.int32) % NZ

    def moved(offset):
        return lax.slice_in_dim(padded, margin + offset, margin + offset + span, axis=2)

    def z_term(offset):
        inside = ((z_pos + offset >= 0) & (z_pos + offset < NZ)).astype(jnp.float32)
        return moved(offset) * inside

    along_z = (
        -2.5 * center + 4.0 / 3.0 * (z_term(1) + z_term(-1)) - 1.0 / 12.0 * (z_term(2) + z_term(-2))
    )
    along_y = (
        -2.5 * center
        + 4.0 / 3.0 * (moved(NZ) + moved(-NZ))
        - 1.0 / 12.0 * (moved(2 * NZ) + moved(-2 * NZ))
    )
    return -0.5 * (along_y + along_z)


def energy(center, plus_one, minus_one, plus_two, minus_two, local_pot):
    along_x = -0.5 * (
        -2.5 * center + 4.0 / 3.0 * (plus_one + minus_one) - 1.0 / 12.0 * (plus_two + minus_two)
    )
    return local_pot * center + along_x + plane_part(center)


def on_device(orbitals, potential, plan, owners):
    band_width = orbitals.shape[0]
    group_count = lax.axis_size("band")
    planes = orbitals.shape[1] // group_count
    norm_factor = 1.0 / math.sqrt(orbitals.shape[1] * orbitals.shape[2])

    def whole_apply(values):
        length = values.shape[1]
        padded = jnp.pad(values, ((0, 0), (2, 2), (0, 0)))
        return energy(
            values,
            padded[:, 3 : 3 + length],
            padded[:, 1 : 1 + length],
            padded[:, 4 : 4 + length],
            padded[:, 0:length],
            potential,
        )

    filtered = chebyshev_filter(orbitals.astype(jnp.float32), whole_apply).astype(jnp.bfloat16)
    slab_orbitals = lax.all_to_all(filtered, "band", split_axis=1, concat_axis=0, tiled=True)
    padded = with_halo(slab_orbitals, (("band", 1),), 2).astype(jnp.float32)
    slab_pot = lax.dynamic_slice_in_dim(potential, lax.axis_index("band") * planes, planes, 0)
    slab_applied = energy(
        padded[:, 2 : 2 + planes],
        padded[:, 3 : 3 + planes],
        padded[:, 1 : 1 + planes],
        padded[:, 4 : 4 + planes],
        padded[:, 0:planes],
        slab_pot,
    ).astype(jnp.bfloat16)
    orbital_groups = slab_orbitals.reshape(group_count, band_width, -1)
    applied_groups = slab_applied.reshape(group_count, band_width, -1)
    collected = []
    for round_index in range(ROUNDS):
        inverse = jnp.argsort(owners[round_index])
        partner = plan[round_index]
        left_block = jnp.take(orbital_groups, inverse, axis=0)
        right_block = jnp.take(applied_groups, jnp.take(partner, inverse), axis=0)
        product = jnp.einsum(
            "kac,kbc->kab", left_block, right_block, preferred_element_type=jnp.float32
        )
        collected.append(
            lax.psum_scatter(
                (product * norm_factor).reshape(band_width * lax.axis_size("band"), band_width),
                "band",
                scatter_dimension=0,
                tiled=True,
            )
        )
    tiles = jnp.stack(collected)
    return (filtered, tiles)


def solution(mesh):
    placed = (
        P(("groups", "band"), None, None),
        P("groups", None),
        P("groups", None),
        P("groups", None),
    )
    return jax.shard_map(
        on_device,
        mesh=mesh,
        in_specs=placed,
        out_specs=(P(("groups", "band"), None, None), P(None, ("groups", "band"), None)),
        check_vma=False,
    )
```

profile of v0, /device:TPU:0, one launch (start us, length us, event | category | flops | bytes accessed | tf_op | source)
XLA Modules:
  0.0 194.6 jit_solution(11361527517866755214)
XLA Ops:
  7.2 0.0 copy-start.1
  7.2 1.3 copy_convert_fusion
  8.5 0.0 copy-done.1
  8.5 0.0 copy-start
  8.5 2.9 %broadcast_multiply_fusion = (f32[80,32,128]{2,0,1:T(8,128)S(1)}, f32[80,32,128]{2,0,1:T(8,128)S(1)}) fusion(f32[80,32,128]{2,0,1:T(8,128)S(1)} %copy_convert_fusion, f32[128]{0:T(128)S(1)} %get-tuple-element.22, f32[128]{0:T(128)S(1)} %get-tuple-element.23, f32[128]{0:T(128)S(1)} %get-tuple-element.24, f32[128]{0:T(128)S(1)} %get-tuple-element.25, ...), kind=kLoop, calls=%fused_computation.134 | loop fusion | flops 10485760 | bytes 3950592 | tf_op jit(solution)/shard_map/mul | solution.py:35
  11.4 0.0 copy-done
  11.5 3.7 %fusion.20 = bf16[80,32,128]{2,0,1:T(8,128)(2,1)} fusion(f32[80,32,128]{2,0,1:T(8,128)S(1)} %get-tuple-element.16, f32[80,32,128]{2,0,1:T(8,128)S(1)} %get-tuple-element.17, f32[32,128]{1,0:T(8,128)S(1)} %broadcast_multiply_fusion.1, f32[128]{0:T(128)S(1)} %get-tuple-element.22, f32[128]{0:T(128)S(1)} %get-tuple-element.23, f32[128]{0:T(128)S(1)} %get-tuple-element.24, ...), kind=kLoop, calls=%fused_computation.59 | loop fusion | flops 11796480 | bytes 3950592 | tf_op jit(solution)/shard_map/convert_element_type | solution.py:95
  15.2 0.0 copy-start.2
  15.2 0.0 copy-start.3
  15.2 7.5 %all-to-all-start = ((bf16[80,32,128]{2,0,1:T(8,128)(2,1)}), bf16[80,32,128]{2,0,1:T(8,128)(2,1)S(1)}, u32[]{:S(2)}, u32[]{:S(2)}) async-start(bf16[80,32,128]{2,0,1:T(8,128)(2,1)} %fusion.20), calls=%async_computation | async-start | bytes 1310720 | tf_op jit(solution)/shard_map/all_to_all | solution.py:96
  22.7 0.0 reduce-scatter.3.cloned.1.call-start
  22.8 0.0 copy-done.2
  22.8 1.2 sort.31
  24.1 0.0 copy-done.3
  24.1 0.7 gather_fusion.1
  24.8 1.3 sort.32
  26.0 13.3 %all-to-all-done = bf16[80,32,128]{2,0,1:T(8,128)(2,1)S(1)} async-done(((bf16[80,32,128]{2,0,1:T(8,128)(2,1)}), bf16[80,32,128]{2,0,1:T(8,128)(2,1)S(1)}, u32[]{:S(2)}, u32[]{:S(2)}) %all-to-all-start) | async-done | bytes 655392 | tf_op jit(solution)/shard_map/all_to_all | solution.py:96
  39.3 2.1 %collective-permute-start = (bf16[1280,2,128]{2,0,1:T(8,128)(2,1)S(1)}, bf16[1280,2,128]{2,0,1:T(8,128)(2,1)S(1)}, u32[]{:S(2)}, u32[]{:S(2)}) collective-permute-start(bf16[1280,2,128]{2,0,1:T(8,128)(2,1)S(1)} %bitcast.24), channel_id=1, source_target_pairs={{0,1},{1,2},{2,3},{3,4},{4,5},{5,6},{6,7},{7,8},{8,9},{9,10},{10,1... | collective-permute-start | bytes 1966088 | tf_op jit(solution)/shard_map/ppermute | solution.py:26
  41.5 1.3 collective-permute-start.1
  42.8 0.1 copy.17
  43.0 0.6 gather_fusion
  43.5 0.0 collective-permute-done
  43.6 2.1 %collective-permute-done.1 = bf16[1280,2,128]{2,0,1:T(8,128)(2,1)} collective-permute-done((bf16[1280,2,128]{2,0,1:T(8,128)(2,1)S(1)}, bf16[1280,2,128]{2,0,1:T(8,128)(2,1)}, u32[]{:S(2)}, u32[]{:S(2)}) %collective-permute-start.1) | collective-permute-done | bytes 655392 | tf_op jit(solution)/shard_map/ppermute | solution.py:27
  45.6 1.4 maximum_convert_fusion
  47.0 0.1 slice.176
  47.1 2.9 %fusion.66 = bf16[1280,2,128]{2,0,1:T(8,128)(2,1)S(1)} fusion(f32[1280,2,128]{2,0,1:T(8,128)S(1)} %slice.176, f32[1280,6,128]{2,0,1:T(8,128)S(1)} %maximum_convert_fusion, f32[128]{0:T(128)S(1)} %get-tuple-element.22, f32[128]{0:T(128)S(1)} %get-tuple-element.23, f32[128]{0:T(128)S(1)} %get-tuple-element.24, f32[128]{0:T(128)S(1)} %get-tuple-element.25, ...), kind=kLoop, calls=%fused_computation.105 | loop fusion | flops 9830400 | bytes 7212032 | tf_op jit(solution)/shard_map/convert_element_type | solution.py:106
  50.0 5.4 %copy.10 = bf16[1280,2,128]{2,1,0:T(2,128)(2,1)S(1)} copy(bf16[1280,2,128]{2,0,1:T(8,128)(2,1)S(1)} %fusion.66) | data formatting | bytes 1310720 | tf_op jit(solution)/shard_map/convert_element_type | solution.py:106
  55.5 0.4 reshape.65
  55.9 0.6 gather_fusion.2
  56.5 1.3 convolution_multiply_fusion.1
  57.8 0.0 reduce-scatter.3.cloned.1.call-update
  57.8 0.0 reduce-scatter.5.cloned.1.call-start
  57.8 0.7 gather_fusion.4
  58.5 0.6 gather_fusion.3
  59.1 0.6 gather_fusion.5
  59.7 1.3 convolution_multiply_fusion
  61.0 0.0 reduce-scatter.5.cloned.1.call-update
  61.0 2.1 %copy.11 = bf16[80,32,128]{2,1,0:T(8,128)(2,1)} copy(bf16[80,32,128]{2,0,1:T(8,128)(2,1)} %fusion.20) | data formatting | bytes 1310720
  63.1 64.1 %reduce-scatter.3.cloned.1.call-done = f32[80,80]{1,0:T(8,128)} async-done(((f32[1280,80]{1,0:T(8,128)}), f32[80,80]{1,0:T(8,128)}) %reduce-scatter.3.cloned.1.call-update) | async-done | bytes 25616 | tf_op jit(solution)/shard_map/reduce_scatter | solution.py:119
  127.2 59.1 %reduce-scatter.5.cloned.1.call-done = f32[80,80]{1,0:T(8,128)} async-done(((f32[1280,80]{1,0:T(8,128)}), f32[80,80]{1,0:T(8,128)}) %reduce-scatter.5.cloned.1.call-update) | async-done | bytes 25616 | tf_op jit(solution)/shard_map/reduce_scatter | solution.py:119
  186.3 1.4 pad_maximum_fusion
  (17 shorter events, 0.2 us)
Async XLA Ops:
  7.2 1.3 copy-start.1
  8.5 2.9 %copy-start = (bf16[80,32,128]{2,1,0:T(8,128)(2,1)S(1)}, bf16[80,32,128]{2,1,0:T(8,128)(2,1)}, u32[]{:S(2)}) copy-start(bf16[80,32,128]{2,1,0:T(8,128)(2,1)} %param.8) | copy-start | bytes 1966084
  15.2 7.6 %copy-start.2 = (s32[2,16]{1,0:T(2,128)S(1)}, s32[2,16]{1,0:T(2,128)}, u32[]{:S(2)}) copy-start(s32[2,16]{1,0:T(2,128)} %param.11) | copy-start | bytes 388
  15.2 8.9 %copy-start.3 = (s32[2,16]{1,0:T(2,128)S(1)}, s32[2,16]{1,0:T(2,128)}, u32[]{:S(2)}) copy-start(s32[2,16]{1,0:T(2,128)} %param.10) | copy-start | bytes 388
  15.2 24.1 %all-to-all-start = ((bf16[80,32,128]{2,0,1:T(8,128)(2,1)}), bf16[80,32,128]{2,0,1:T(8,128)(2,1)S(1)}, u32[]{:S(2)}, u32[]{:S(2)}) async-start(bf16[80,32,128]{2,0,1:T(8,128)(2,1)} %fusion.20), calls=%async_computation | async-start | bytes 1310720 | tf_op jit(solution)/shard_map/all_to_all | solution.py:96
  22.7 104.5 %reduce-scatter.3.cloned.1.call-start = ((), (), s32[]{:S(2)}) async-start(), calls=%async_computation.3 | async-start | bytes 696320 | tf_op jit(solution)/shard_map/reduce_scatter | solution.py:119
  39.3 4.2 %collective-permute-start = (bf16[1280,2,128]{2,0,1:T(8,128)(2,1)S(1)}, bf16[1280,2,128]{2,0,1:T(8,128)(2,1)S(1)}, u32[]{:S(2)}, u32[]{:S(2)}) collective-permute-start(bf16[1280,2,128]{2,0,1:T(8,128)(2,1)S(1)} %bitcast.24), channel_id=1, source_target_pairs={{0,1},{1,2},{2,3},{3,4},{4,5},{5,6},{6,7},{7,8},{8,9},{9,10},{10,1... | collective-permute-start | bytes 1966088 | tf_op jit(solution)/shard_map/ppermute | solution.py:26
  41.5 4.2 %collective-permute-start.1 = (bf16[1280,2,128]{2,0,1:T(8,128)(2,1)S(1)}, bf16[1280,2,128]{2,0,1:T(8,128)(2,1)}, u32[]{:S(2)}, u32[]{:S(2)}) collective-permute-start(bf16[1280,2,128]{2,0,1:T(8,128)(2,1)S(1)} %bitcast.25), channel_id=1, source_target_pairs={{1,0},{2,1},{3,2},{4,3},{5,4},{6,5},{7,6},{8,7},{9,8},{10,9},{11,1... | collective-permute-start | bytes 1966088 | tf_op jit(solution)/shard_map/ppermute | solution.py:27
  57.8 128.6 %reduce-scatter.5.cloned.1.call-start = ((), (), s32[]{:S(2)}) async-start(), calls=%async_computation.4 | async-start | bytes 696320 | tf_op jit(solution)/shard_map/reduce_scatter | solution.py:119
Sparse Core Ops, SparseCore 0:
  57.9 69.2 reduce-scatter.2
  130.7 55.5 reduce-scatter.4
where the time goes:
time: 195 us
  waiting for transfers between devices  139 us (71%)
  other arithmetic  16.2 us (8%)
  between operations  14.3 us (7%)
  local copies, waits for them, and re-layouts  11.9 us (6%)
  starting transfers between devices  11 us (6%)
  matrix products  2.55 us (1%)
    reduce_scatter x2, waiting for transfers between devices, on_device(): lax.psum_scatter((product * norm_factor).reshape(band_width * lax.axis_si...  123 us
    all_to_all x1, waiting for transfers between devices, on_device(): lax.all_to_all(filtered, 'band', split_axis=1, concat_axis=0, tiled=True)  13.3 us
    all_to_all x1, starting transfers between devices, on_device(): lax.all_to_all(filtered, 'band', split_axis=1, concat_axis=0, tiled=True)  7.55 us
    convert_element_type x1, local copies, waits for them, and re-layouts, on_device(): slab_applied = energy(padded[:, 2:2 + planes], padded[:, 3:3 + planes], p...  5.44 us
  transfers between devices with their start and end apart: 5, of which 4 were waited for; matrix products, arithmetic and copies ran while one was open for 5% of the time, Pallas kernels for 0%

commit v1 on v0

v1 whole, which is shorter than its diff:
```python
import functools
import math

import jax
import jax.numpy as jnp
from jax import lax
from jax.experimental import pallas as pl
from jax.experimental.pallas import tpu as pltpu
from jax.sharding import PartitionSpec as P

NZ = 16
ROUNDS = 2
CHUNK = 16
BLOCK = 8

lower_edge = -2.5
cutoff_edge = 4.0
upper_edge = 8.5
half_width = (upper_edge - cutoff_edge) / 2.0
middle_point = (upper_edge + cutoff_edge) / 2.0
sigma_zero = half_width / (lower_edge - middle_point)
sigma_next = 1.0 / (2.0 / sigma_zero - sigma_zero)
first_scale = sigma_zero / half_width
second_scale = 2.0 * sigma_next / half_width
back_scale = sigma_zero * sigma_next


def plane_matrix():
    row = lax.broadcasted_iota(jnp.int32, (128, 128), 0)
    col = lax.broadcasted_iota(jnp.int32, (128, 128), 1)
    gap = jnp.abs(row - col)
    same = (row // NZ) == (col // NZ)
    near = (same & (gap == 1)) | (gap == NZ)
    far = (same & (gap == 2)) | (gap == 2 * NZ)
    return jnp.where(
        gap == 0, -90.0, jnp.where(near, 16.0, jnp.where(far, -1.0, 0.0))
    ).astype(jnp.bfloat16)


def body(
    n, orb, pot, plan, owners, filt, tiles,
    wide, y0, y1, fil, matrix, send, recv, part, gathered, inverse,
    send_sem, recv_sem, relay_send, relay_recv, part_send, part_recv,
):
    me = lax.axis_index("band")
    core = lax.rem(me, 2)
    chip = me // 2
    chips = n // 2
    other = me + 1 - 2 * core
    bands, nx = orb.shape[0], orb.shape[1]
    chunks = bands // CHUNK
    planes = nx // n
    norm = 1.0 / math.sqrt(nx * orb.shape[2])

    barrier = pltpu.get_barrier_semaphore()

    def greet(o, c):
        pl.semaphore_signal(barrier, inc=1, device_id={"band": lax.rem(me + o, n)})
        return c

    lax.fori_loop(1, n, greet, 0)

    def walk(_, c):
        a, b, am, bm = c
        a = plan[1, plan[0, a]]
        b = plan[1, plan[0, b]]
        return a, b, jnp.minimum(am, a), jnp.minimum(bm, b)

    b0 = plan[0, me]
    _, _, am, bm = lax.fori_loop(0, n // 2, walk, (me, b0, me, b0))
    plain = am < bm

    matrix[...] = plane_matrix()
    edge = jnp.zeros((2, CHUNK, 128), jnp.float32)
    for buf in (y0, y1, fil):
        buf[0:2] = edge
        buf[nx + 2 : nx + 4] = edge

    def lap(buf, start, split):
        v = buf[pl.ds(start, BLOCK + 4)]
        mid = v[2 : 2 + BLOCK].reshape(BLOCK * CHUNK, 128)
        high = mid.astype(jnp.bfloat16)
        m = matrix[...]
        out = jnp.dot(high, m, preferred_element_type=jnp.float32)
        if split:
            low = (mid - high.astype(jnp.float32)).astype(jnp.bfloat16)
            out = out + jnp.dot(low, m, preferred_element_type=jnp.float32)
        out = out.reshape(BLOCK, CHUNK, 128)
        out = out + 16.0 * (v[1 : 1 + BLOCK] + v[3 : 3 + BLOCK])
        out = out - (v[0:BLOCK] + v[4 : 4 + BLOCK])
        return v[2 : 2 + BLOCK], out * (1.0 / 24.0)

    def local_pot(start):
        return pot[pl.ds(start, BLOCK), :].reshape(BLOCK, 1, 128)

    blocks = nx // BLOCK

    def each_block(fn):
        if blocks <= 4:
            for b in range(blocks):
                fn(b * BLOCK)
        else:
            def step(b, c):
                fn(pl.multiple_of(b * BLOCK, BLOCK))
                return c

            lax.fori_loop(0, blocks, step, 0)

    def one_chunk(ch, c):
        base = pl.multiple_of(ch * CHUNK, CHUNK)
        wide[...] = orb[pl.ds(base, CHUNK)].astype(jnp.float32).reshape(CHUNK * nx, 128)

        def take(start):
            for j in range(BLOCK):
                y0[start + 2 + j] = wide[pl.ds(start + j, CHUNK, stride=nx), :]

        each_block(take)

        def first(start):
            v, l = lap(y0, start, False)
            y1[pl.ds(start + 2, BLOCK)] = first_scale * ((local_pot(start) - middle_point) * v - l)

        each_block(first)

        def second(start):
            v, l = lap(y1, start, True)
            f = second_scale * ((local_pot(start) - middle_point) * v - l) - back_scale * y0[
                pl.ds(start + 2, BLOCK)
            ]
            f = f.astype(jnp.bfloat16).astype(jnp.float32)
            fil[pl.ds(start + 2, BLOCK)] = f
            for j in range(BLOCK):
                wide[pl.ds(start + j, CHUNK, stride=nx), :] = f[j]

        each_block(second)
        filt[pl.ds(base, CHUNK)] = wide[...].reshape(CHUNK, nx, 128).astype(jnp.bfloat16)

        def third(start):
            v, l = lap(fil, start, False)
            x = jnp.where(plain, v, local_pot(start) * v - l).astype(jnp.bfloat16)
            for q in range(BLOCK // planes):
                for j in range(planes):
                    send[ch, start // planes + q, :, j * 128 : (j + 1) * 128] = x[q * planes + j]

        each_block(third)

        @pl.when(ch == 0)
        def _():
            pl.semaphore_wait(barrier, n - 1)

        def push(o, c):
            d = lax.rem(me + o, n)
            pltpu.make_async_remote_copy(
                src_ref=send.at[ch, d],
                dst_ref=recv.at[lax.rem(d, 2), ch, me],
                send_sem=send_sem.at[ch],
                recv_sem=recv_sem.at[ch],
                device_id={"band": d},
            ).start()
            return c

        lax.fori_loop(1, n, push, 0)
        recv[core, ch, me] = send[ch, me]
        return c

    lax.fori_loop(0, chunks, one_chunk, 0)

    for r in range(ROUNDS):
        def find(j, c, r=r):
            d = 2 * j + core

            def look(i, found):
                return jnp.where(owners[r, i] == d, i, found)

            inverse[r, j] = lax.fori_loop(0, n, look, jnp.int32(0), unroll=8)
            return c

        lax.fori_loop(0, chips, find, 0)

    def all_but_one(ch):
        return pltpu.make_async_remote_copy(
            src_ref=send.at[ch, 0 : n - 1],
            dst_ref=recv.at[core, ch, 0 : n - 1],
            send_sem=send_sem.at[ch],
            recv_sem=recv_sem.at[ch],
            device_id={"band": other},
        )

    def relay(ch):
        return pltpu.make_async_remote_copy(
            src_ref=recv.at[core, ch],
            dst_ref=recv.at[core, ch],
            send_sem=relay_send.at[ch],
            recv_sem=relay_recv.at[ch],
            device_id={"band": other},
        )

    for ch in range(chunks):
        all_but_one(ch).wait_recv()
        relay(ch).start()
    for ch in range(chunks):
        pltpu.make_async_remote_copy(
            src_ref=recv.at[core, ch],
            dst_ref=recv.at[1 - core, ch],
            send_sem=relay_send.at[ch],
            recv_sem=relay_recv.at[ch],
            device_id={"band": other},
        ).wait_recv()

    def tile(r, j):
        i = inverse[r, j]
        p = plan[r, i]
        total = jnp.zeros((bands, bands), jnp.float32)
        for half in range(2):
            left = recv[half, :, i].reshape(bands, planes * 128)
            right = recv[half, :, p].reshape(bands, planes * 128)
            total = total + lax.dot_general(
                left, right, (((1,), (1,)), ((), ())), preferred_element_type=jnp.float32
            )
        return total * norm

    def produce(o, c):
        j = lax.rem(chip + o, chips)
        for r in range(ROUNDS):
            part[j, r] = tile(r, j).astype(jnp.bfloat16)
        pltpu.make_async_remote_copy(
            src_ref=part.at[j],
            dst_ref=gathered.at[chip],
            send_sem=part_send,
            recv_sem=part_recv,
            device_id={"band": 2 * j + core},
        ).start()
        return c

    lax.fori_loop(1, chips, produce, 0)
    for r in range(ROUNDS):
        tiles[r] = tile(r, chip)
    gathered[chip] = jnp.zeros((ROUNDS, bands, bands), jnp.bfloat16)
    last = pltpu.make_async_remote_copy(
        src_ref=part.at[0 : chips - 1],
        dst_ref=gathered.at[0 : chips - 1],
        send_sem=part_send,
        recv_sem=part_recv,
        device_id={"band": other},
    )
    last.wait_recv()

    def add(s, c):
        for r in range(ROUNDS):
            tiles[r] += gathered[s, r].astype(jnp.float32)
        return c

    lax.fori_loop(0, chips, add, 0)

    last.wait_send()
    for ch in range(chunks):
        all_but_one(ch).wait_send()
        relay(ch).wait_send()


def on_device(orbitals, potential, plan, owners):
    n = lax.axis_size("band")
    bands, nx, cells = orbitals.shape
    chunks, planes = bands // CHUNK, nx // n
    vmem = pl.BlockSpec(memory_space=pltpu.VMEM)
    smem = pl.BlockSpec(memory_space=pltpu.SMEM)
    dma = pltpu.SemaphoreType.DMA
    return pl.pallas_call(
        functools.partial(body, n),
        out_shape=(
            jax.ShapeDtypeStruct((bands, nx, cells), jnp.bfloat16),
            jax.ShapeDtypeStruct((ROUNDS, bands, bands), jnp.float32),
        ),
        in_specs=[vmem, vmem, smem, smem],
        out_specs=(vmem, vmem),
        scratch_shapes=[
            pltpu.VMEM((CHUNK * nx, 128), jnp.float32),
            pltpu.VMEM((nx + 4, CHUNK, 128), jnp.float32),
            pltpu.VMEM((nx + 4, CHUNK, 128), jnp.float32),
            pltpu.VMEM((nx + 4, CHUNK, 128), jnp.float32),
            pltpu.VMEM((128, 128), jnp.bfloat16),
            pltpu.VMEM((chunks, n, CHUNK, planes * 128), jnp.bfloat16),
            pltpu.VMEM((2, chunks, n, CHUNK, planes * 128), jnp.bfloat16),
            pltpu.VMEM((n // 2, ROUNDS, bands, bands), jnp.bfloat16),
            pltpu.VMEM((n // 2, ROUNDS, bands, bands), jnp.bfloat16),
            pltpu.SMEM((ROUNDS, n // 2), jnp.int32),
            dma((chunks,)),
            dma((chunks,)),
            dma((chunks,)),
            dma((chunks,)),
            dma,
            dma,
        ],
        compiler_params=pltpu.CompilerParams(collective_id=0, has_side_effects=True),
    )(orbitals, potential, plan, owners)


def solution(mesh):
    placed = (
        P(("groups", "band"), None, None),
        P("groups", None),
        P("groups", None),
        P("groups", None),
    )
    return jax.shard_map(
        on_device,
        mesh=mesh,
        in_specs=placed,
        out_specs=(P(("groups", "band"), None, None), P(None, ("groups", "band"), None)),
        check_vma=False,
    )
```

time: 195 us -> 36.9 us (0.19)
  waiting for transfers between devices: 139 us -> 0 us
  Pallas kernels: 0 us -> 33.5 us
  other arithmetic: 16.2 us -> 0 us
  between operations: 14.3 us -> 0.65 us
  starting transfers between devices: 11 us -> 0 us
  local copies, waits for them, and re-layouts: 11.9 us -> 2.64 us
  matrix products: 2.55 us -> 0 us
    reduce_scatter x2 -> x0, waiting for transfers between devices: 123 us -> none  [on_device(): lax.psum_scatter((product * norm_factor).reshape(band_width * lax.axis_si...]
    pallas_call x0 -> x1, Pallas kernels: none -> 33.5 us  [on_device(): pl.pallas_call(functools.partial(body, n), out_shape=(jax.ShapeDtypeStruc...]
    all_to_all x1 -> x0, waiting for transfers between devices: 13.3 us -> none  [on_device(): lax.all_to_all(filtered, 'band', split_axis=1, concat_axis=0, tiled=True)]
    convert_element_type x6 -> x0, other arithmetic: 9.29 us -> none  [the longest x1 3.71 us: on_device(): chebyshev_filter(orbitals.astype(jnp.float32), whole_apply)]
    all_to_all x1 -> x0, starting transfers between devices: 7.55 us -> none  [on_device(): lax.all_to_all(filtered, 'band', split_axis=1, concat_axis=0, tiled=True)]
    convert_element_type x1 -> x0, local copies, waits for them, and re-layouts: 5.44 us -> none  [on_device(): slab_applied = energy(padded[:, 2:2 + planes], padded[:, 3:3 + planes], p...]
    gather x6 -> x0, local copies, waits for them, and re-layouts: 3.67 us -> none  [the longest x4 2.49 us: on_device(): right_block = jnp.take(applied_groups, jnp.take(partner, inverse), axis=0)]
    ppermute x2 -> x0, starting transfers between devices: 3.41 us -> none  [the longest x1 2.12 us: with_halo(): before = lax.ppermute(last, axis, up)]
  transfers between devices with their start and end apart: 5 -> 0, of which waited for: 4 -> 0; matrix products, arithmetic and copies ran while one was open for 5% -> 0% of each run, Pallas kernels for 0% -> 0%
where the time goes in v1:
time: 36.9 us; the launch traced here: 36.7 us
  Pallas kernels  33.5 us (91%)
  local copies, waits for them, and re-layouts  2.64 us (7%)
  between operations  0.65 us (2%)
    pallas_call x1, Pallas kernels, on_device(): pl.pallas_call(functools.partial(body, n), out_shape=(jax.ShapeDtypeStruc...  33.5 us
    unnamed x4, local copies, waits for them, and re-layouts  2.64 us

profile of v1, /device:TPU:0, one launch (start us, length us, event | category | flops | bytes accessed | tf_op | source)
XLA Modules:
  0.0 36.7 jit_solution(17243803343711333695)
XLA Ops:
  0.6 33.5 %shard_map.59 = (bf16[80,32,128]{2,1,0:T(8,128)(2,1)}, f32[2,80,80]{2,1,0:T(8,128)}) custom-call(bf16[80,32,128]{2,1,0:T(8,128)(2,1)} %orb.1, f32[32,128]{1,0:T(8,128)} %pot.1, s32[2,16]{1,0:T(2,128)} %plan.1, s32[2,16]{1,0:T(2,128)} %owners.1), custom_call_target="tpu_custom_call" | custom-call | tf_op jit(solution)/shard_map/pallas_call | solution.py:268
  34.1 0.0 copy-start
  34.1 2.0 %copy.8 = bf16[80,32,128]{2,1,0:T(8,128)(2,1)} copy(bf16[80,32,128]{2,1,0:T(8,128)(2,1)} %get-tuple-element.4) | data formatting | bytes 1310720
  36.1 0.0 copy-done
  36.1 0.6 %copy.9 = f32[2,80,80]{2,1,0:T(8,128)} copy(f32[2,80,80]{2,1,0:T(8,128)S(1)} %copy-done) | data formatting | bytes 102400
Async XLA Ops:
  34.1 2.0 %copy-start = (f32[2,80,80]{2,1,0:T(8,128)S(1)}, f32[2,80,80]{2,1,0:T(8,128)}, u32[]{:S(2)}) copy-start(f32[2,80,80]{2,1,0:T(8,128)} %get-tuple-element.5) | copy-start | bytes 153604

commit v2 on v1

--- a/solution.py
+++ b/solution.py
@@ -207,22 +207,51 @@
             device_id={"band": other},
         ).wait_recv()
 
-    def tile(r, j):
+    lead = 128 - bands
+    tail = bands - lead
+    strips = -(-bands // tail)
+    lanes = lax.broadcasted_iota(jnp.int32, (bands, 128), 1)
+    tail_lanes = lax.broadcasted_iota(jnp.int32, (tail, 128), 1)
+
+    def product(r, j):
         i = inverse[r, j]
         p = plan[r, i]
-        total = jnp.zeros((bands, bands), jnp.float32)
+        blank = jnp.zeros((lead, planes * 128), jnp.bfloat16)
+        total = None
         for half in range(2):
             left = recv[half, :, i].reshape(bands, planes * 128)
             right = recv[half, :, p].reshape(bands, planes * 128)
-            total = total + lax.dot_general(
+            if r == 0:
+                right = jnp.concatenate([right, blank], axis=0)
+            else:
+                right = jnp.concatenate([right[lead:], blank, right[:lead]], axis=0)
+            term = lax.dot_general(
                 left, right, (((1,), (1,)), ((), ())), preferred_element_type=jnp.float32
             )
+            total = term if total is None else total + term
         return total * norm
+
+    def packed(j):
+        one, two = product(0, j), product(1, j)
+        top = jnp.where(lanes < bands, one, two)
+        low = jnp.zeros((tail, 128), jnp.float32)
+        for q in range(strips):
+            rows = two[q * tail : min(bands, (q + 1) * tail)]
+            if rows.shape[0] < tail:
+                rows = jnp.concatenate(
+                    [rows, jnp.zeros((tail - rows.shape[0], 128), jnp.float32)], axis=0
+                )
+            if q > 0:
+                rows = pltpu.roll(rows, q * tail, 1)
+            here = (tail_lanes >= q * tail) & (tail_lanes < (q + 1) * tail)
+            low = jnp.where(here, rows, low)
+        return top, low
 
     def produce(o, c):
         j = lax.rem(chip + o, chips)
-        for r in range(ROUNDS):
-            part[j, r] = tile(r, j).astype(jnp.bfloat16)
+        top, low = packed(j)
+        part[j, 0:bands] = top.astype(jnp.bfloat16)
+        part[j, bands : bands + tail] = low.astype(jnp.bfloat16)
         pltpu.make_async_remote_copy(
             src_ref=part.at[j],
             dst_ref=gathered.at[chip],
@@ -232,10 +261,10 @@
         ).start()
         return c
 
-    lax.fori_loop(1, chips, produce, 0)
-    for r in range(ROUNDS):
-        tiles[r] = tile(r, chip)
-    gathered[chip] = jnp.zeros((ROUNDS, bands, bands), jnp.bfloat16)
+    lax.fori_loop(chips // 2, chips, produce, 0)
+    lax.fori_loop(1, chips // 2, produce, 0)
+    top, low = packed(chip)
+    gathered[chip] = jnp.zeros((bands + tail, 128), jnp.bfloat16)
     last = pltpu.make_async_remote_copy(
         src_ref=part.at[0 : chips - 1],
         dst_ref=gathered.at[0 : chips - 1],
@@ -244,13 +273,26 @@
         device_id={"band": other},
     )
     last.wait_recv()
-
-    def add(s, c):
-        for r in range(ROUNDS):
-            tiles[r] += gathered[s, r].astype(jnp.float32)
-        return c
-
-    lax.fori_loop(0, chips, add, 0)
+    if chips <= 8:
+        for s in range(chips):
+            top = top + gathered[s, 0:bands].astype(jnp.float32)
+            low = low + gathered[s, bands : bands + tail].astype(jnp.float32)
+    else:
+        def add(s, c):
+            return (
+                c[0] + gathered[s, 0:bands].astype(jnp.float32),
+                c[1] + gathered[s, bands : bands + tail].astype(jnp.float32),
+            )
+
+        top, low = lax.fori_loop(0, chips, add, (top, low))
+    tiles[0] = top[:, 0:bands]
+    front = pltpu.roll(top, lead, 1)
+    backs = []
+    for q in range(strips):
+        rows = pltpu.roll(low, (lead - q * tail) % 128, 1) if lead != q * tail else low
+        backs.append(rows[0 : min(tail, bands - q * tail)])
+    back = jnp.concatenate(backs, axis=0)
+    tiles[1] = jnp.where(lanes < lead, front, back)[:, 0:bands]
 
     last.wait_send()
     for ch in range(chunks):
@@ -281,8 +323,8 @@
             pltpu.VMEM((128, 128), jnp.bfloat16),
             pltpu.VMEM((chunks, n, CHUNK, planes * 128), jnp.bfloat16),
             pltpu.VMEM((2, chunks, n, CHUNK, planes * 128), jnp.bfloat16),
-            pltpu.VMEM((n // 2, ROUNDS, bands, bands), jnp.bfloat16),
-            pltpu.VMEM((n // 2, ROUNDS, bands, bands), jnp.bfloat16),
+            pltpu.VMEM((n // 2, 2 * bands - (128 - bands), 128), jnp.bfloat16),
+            pltpu.VMEM((n // 2, 2 * bands - (128 - bands), 128), jnp.bfloat16),
             pltpu.SMEM((ROUNDS, n // 2), jnp.int32),
             dma((chunks,)),
             dma((chunks,)),

time: 36.9 us -> 35.9 us (0.973)
  Pallas kernels: 33.5 us -> 32.4 us
    pallas_call x1, Pallas kernels: 33.5 us -> 32.4 us  [on_device(): pl.pallas_call(functools.partial(body, n), out_shape=(jax.ShapeDtypeStruc...]
where the time goes in v2:
time: 35.9 us; the launch traced here: 35.7 us
  Pallas kernels  32.4 us (90%)
  local copies, waits for them, and re-layouts  2.64 us (7%)
  between operations  0.65 us (2%)
    pallas_call x1, Pallas kernels, on_device(): pl.pallas_call(functools.partial(body, n), out_shape=(jax.ShapeDtypeStruc...  32.4 us
    unnamed x4, local copies, waits for them, and re-layouts  2.64 us

profile of v2, /device:TPU:0, one launch (start us, length us, event | category | flops | bytes accessed | tf_op | source)
XLA Modules:
  0.0 35.7 jit_solution(16499449736173590066)
XLA Ops:
  0.6 32.4 %shard_map.59 = (bf16[80,32,128]{2,1,0:T(8,128)(2,1)}, f32[2,80,80]{2,1,0:T(8,128)}) custom-call(bf16[80,32,128]{2,1,0:T(8,128)(2,1)} %orb.1, f32[32,128]{1,0:T(8,128)} %pot.1, s32[2,16]{1,0:T(2,128)} %plan.1, s32[2,16]{1,0:T(2,128)} %owners.1), custom_call_target="tpu_custom_call" | custom-call | tf_op jit(solution)/shard_map/pallas_call | solution.py:310
  33.1 0.0 copy-start
  33.1 2.0 %copy.8 = bf16[80,32,128]{2,1,0:T(8,128)(2,1)} copy(bf16[80,32,128]{2,1,0:T(8,128)(2,1)} %get-tuple-element.4) | data formatting | bytes 1310720
  35.1 0.0 copy-done
  35.1 0.6 %copy.9 = f32[2,80,80]{2,1,0:T(8,128)} copy(f32[2,80,80]{2,1,0:T(8,128)S(1)} %copy-done) | data formatting | bytes 102400
Async XLA Ops:
  33.1 2.0 %copy-start = (f32[2,80,80]{2,1,0:T(8,128)S(1)}, f32[2,80,80]{2,1,0:T(8,128)}, u32[]{:S(2)}) copy-start(f32[2,80,80]{2,1,0:T(8,128)} %get-tuple-element.5) | copy-start | bytes 153604

commit v3 on v2

--- a/solution.py
+++ b/solution.py
@@ -140,30 +140,30 @@
             x = jnp.where(plain, v, local_pot(start) * v - l).astype(jnp.bfloat16)
             for q in range(BLOCK // planes):
                 for j in range(planes):
-                    send[ch, start // planes + q, :, j * 128 : (j + 1) * 128] = x[q * planes + j]
+                    send[
+                        start // planes + q, pl.ds(base, CHUNK), j * 128 : (j + 1) * 128
+                    ] = x[q * planes + j]
 
         each_block(third)
 
-        @pl.when(ch == 0)
-        def _():
-            pl.semaphore_wait(barrier, n - 1)
-
-        def push(o, c):
-            d = lax.rem(me + o, n)
-            pltpu.make_async_remote_copy(
-                src_ref=send.at[ch, d],
-                dst_ref=recv.at[lax.rem(d, 2), ch, me],
-                send_sem=send_sem.at[ch],
-                recv_sem=recv_sem.at[ch],
-                device_id={"band": d},
-            ).start()
-            return c
-
-        lax.fori_loop(1, n, push, 0)
-        recv[core, ch, me] = send[ch, me]
         return c
 
     lax.fori_loop(0, chunks, one_chunk, 0)
+    pl.semaphore_wait(barrier, n - 1)
+
+    def push(o, c):
+        d = lax.rem(me + o, n)
+        pltpu.make_async_remote_copy(
+            src_ref=send.at[d],
+            dst_ref=recv.at[lax.rem(d, 2), me],
+            send_sem=send_sem,
+            recv_sem=recv_sem.at[me],
+            device_id={"band": d},
+        ).start()
+        return c
+
+    lax.fori_loop(1, n, push, 0)
+    recv[core, me] = send[me]
 
     for r in range(ROUNDS):
         def find(j, c, r=r):
@@ -177,35 +177,37 @@
 
         lax.fori_loop(0, chips, find, 0)
 
-    def all_but_one(ch):
+    def relay(source):
         return pltpu.make_async_remote_copy(
-            src_ref=send.at[ch, 0 : n - 1],
-            dst_ref=recv.at[core, ch, 0 : n - 1],
-            send_sem=send_sem.at[ch],
-            recv_sem=recv_sem.at[ch],
+            src_ref=recv.at[core, source],
+            dst_ref=recv.at[core, source],
+            send_sem=relay_send,
+            recv_sem=relay_recv,
             device_id={"band": other},
         )
 
-    def relay(ch):
-        return pltpu.make_async_remote_copy(
-            src_ref=recv.at[core, ch],
-            dst_ref=recv.at[core, ch],
-            send_sem=relay_send.at[ch],
-            recv_sem=relay_recv.at[ch],
-            device_id={"band": other},
-        )
-
-    for ch in range(chunks):
-        all_but_one(ch).wait_recv()
-        relay(ch).start()
-    for ch in range(chunks):
+    def pass_on(o, c):
+        source = lax.rem(me + n - o, n)
         pltpu.make_async_remote_copy(
-            src_ref=recv.at[core, ch],
-            dst_ref=recv.at[1 - core, ch],
-            send_sem=relay_send.at[ch],
-            recv_sem=relay_recv.at[ch],
+            src_ref=send.at[0],
+            dst_ref=recv.at[core, source],
+            send_sem=send_sem,
+            recv_sem=recv_sem.at[source],
             device_id={"band": other},
         ).wait_recv()
+        relay(source).start()
+        return c
+
+    relay(me).start()
+    lax.fori_loop(1, n, pass_on, 0)
+    relayed = pltpu.make_async_remote_copy(
+        src_ref=recv.at[core],
+        dst_ref=recv.at[1 - core],
+        send_sem=relay_send,
+        recv_sem=relay_recv,
+        device_id={"band": other},
+    )
+    relayed.wait_recv()
 
     lead = 128 - bands
     tail = bands - lead
@@ -219,8 +221,8 @@
         blank = jnp.zeros((lead, planes * 128), jnp.bfloat16)
         total = None
         for half in range(2):
-            left = recv[half, :, i].reshape(bands, planes * 128)
-            right = recv[half, :, p].reshape(bands, planes * 128)
+            left = recv[half, i]
+            right = recv[half, p]
             if r == 0:
                 right = jnp.concatenate([right, blank], axis=0)
             else:
@@ -295,46 +297,51 @@
     tiles[1] = jnp.where(lanes < lead, front, back)[:, 0:bands]
 
     last.wait_send()
-    for ch in range(chunks):
-        all_but_one(ch).wait_send()
-        relay(ch).wait_send()
+    relayed.wait_send()
+    pltpu.make_async_remote_copy(
+        src_ref=send.at[0 : n - 1],
+        dst_ref=recv.at[core, 0 : n - 1],
+        send_sem=send_sem,
+        recv_sem=recv_sem.at[me],
+        device_id={"band": other},
+    ).wait_send()
 
 
 def on_device(orbitals, potential, plan, owners):
     n = lax.axis_size("band")
     bands, nx, cells = orbitals.shape
-    chunks, planes = bands // CHUNK, nx // n
+    planes = nx // n
     vmem = pl.BlockSpec(memory_space=pltpu.VMEM)
     smem = pl.BlockSpec(memory_space=pltpu.SMEM)
     dma = pltpu.SemaphoreType.DMA
-    return pl.pallas_call(
+    shapes = [((bands, nx, cells), jnp.bfloat16), ((ROUNDS, bands, bands), jnp.float32)]
+    return tuple(pl.pallas_call(
         functools.partial(body, n),
-        out_shape=(
-            jax.ShapeDtypeStruct((bands, nx, cells), jnp.bfloat16),
-            jax.ShapeDtypeStruct((ROUNDS, bands, bands), jnp.float32),
-        ),
+        out_shape=[pltpu.VMEM(shape, dtype) for shape, dtype in shapes],
         in_specs=[vmem, vmem, smem, smem],
-        out_specs=(vmem, vmem),
+        out_specs=[vmem, vmem],
         scratch_shapes=[
             pltpu.VMEM((CHUNK * nx, 128), jnp.float32),
             pltpu.VMEM((nx + 4, CHUNK, 128), jnp.float32),
             pltpu.VMEM((nx + 4, CHUNK, 128), jnp.float32),
             pltpu.VMEM((nx + 4, CHUNK, 128), jnp.float32),
             pltpu.VMEM((128, 128), jnp.bfloat16),
-            pltpu.VMEM((chunks, n, CHUNK, planes * 128), jnp.bfloat16),
-            pltpu.VMEM((2, chunks, n, CHUNK, planes * 128), jnp.bfloat16),
+            pltpu.VMEM((n, bands, planes * 128), jnp.bfloat16),
+            pltpu.VMEM((2, n, bands, planes * 128), jnp.bfloat16),
             pltpu.VMEM((n // 2, 2 * bands - (128 - bands), 128), jnp.bfloat16),
             pltpu.VMEM((n // 2, 2 * bands - (128 - bands), 128), jnp.bfloat16),
             pltpu.SMEM((ROUNDS, n // 2), jnp.int32),
-            dma((chunks,)),
-            dma((chunks,)),
-            dma((chunks,)),
-            dma((chunks,)),
+            dma,
+            dma((n,)),
+            dma,
+            dma,
             dma,
             dma,
         ],
-        compiler_params=pltpu.CompilerParams(collective_id=0, has_side_effects=True),
-    )(orbitals, potential, plan, owners)
+        compiler_params=pltpu.CompilerParams(
+            collective_id=0, has_side_effects=True, vmem_limit_bytes=48 * 2**20
+        ),
+    )(orbitals, potential, plan, owners))
 
 
 def solution(mesh):

time: 35.9 us -> 37.2 us (1.036)
  local copies, waits for them, and re-layouts: 2.64 us -> 4.63 us
  Pallas kernels: 32.4 us -> 31.6 us
    unnamed x4 -> x10, local copies, waits for them, and re-layouts: 2.64 us -> 4.63 us
    pallas_call x1, Pallas kernels: 32.4 us -> 31.6 us  [on_device(): pl.pallas_call(functools.partial(body, n), out_shape=[pltpu.VMEM(shape, d...]
where the time goes in v3:
time: 37.2 us; the launch traced here: 36.9 us
  Pallas kernels  31.6 us (85%)
  local copies, waits for them, and re-layouts  4.63 us (12%)
  between operations  0.65 us (2%)
    pallas_call x1, Pallas kernels, on_device(): pl.pallas_call(functools.partial(body, n), out_shape=[pltpu.VMEM(shape, d...  31.6 us
    unnamed x10, local copies, waits for them, and re-layouts  4.63 us

profile of v3, /device:TPU:0, one launch (start us, length us, event | category | flops | bytes accessed | tf_op | source)
XLA Modules:
  0.0 36.9 jit_solution(18069050525737187994)
XLA Ops:
  0.6 0.0 copy-start
  0.6 1.1 %copy-done = bf16[80,32,128]{2,1,0:T(8,128)(2,1)S(1)} copy-done((bf16[80,32,128]{2,1,0:T(8,128)(2,1)S(1)}, bf16[80,32,128]{2,1,0:T(8,128)(2,1)}, u32[]{:S(2)}) %copy-start) | copy-done | bytes 655384
  1.7 0.0 copy-start.1
  1.7 0.7 %copy-done.1 = f32[32,128]{1,0:T(8,128)S(1)} copy-done((f32[32,128]{1,0:T(8,128)S(1)}, f32[32,128]{1,0:T(8,128)}, u32[]{:S(2)}) %copy-start.1) | copy-done | bytes 16408
  2.4 0.0 copy-start.2
  2.4 0.7 %copy-done.2 = s32[2,16]{1,0:T(2,128)S(1)} copy-done((s32[2,16]{1,0:T(2,128)S(1)}, s32[2,16]{1,0:T(2,128)}, u32[]{:S(2)}) %copy-start.2) | copy-done | bytes 152
  3.1 0.0 copy-start.3
  3.1 0.7 %copy-done.3 = s32[2,16]{1,0:T(2,128)S(1)} copy-done((s32[2,16]{1,0:T(2,128)S(1)}, s32[2,16]{1,0:T(2,128)}, u32[]{:S(2)}) %copy-start.3) | copy-done | bytes 152
  3.8 31.6 %shard_map.59 = (bf16[80,32,128]{2,1,0:T(8,128)(2,1)S(1)}, f32[2,80,80]{2,1,0:T(8,128)S(1)}) custom-call(bf16[80,32,128]{2,1,0:T(8,128)(2,1)S(1)} %copy-done, f32[32,128]{1,0:T(8,128)S(1)} %copy-done.1, s32[2,16]{1,0:T(2,128)S(1)} %copy-done.2, s32[2,16]{1,0:T(2,128)S(1)} %copy-done.3), custom_call_target="tpu_custom_call" | custom-call | tf_op jit(solution)/shard_map/pallas_call | solution.py:318
  35.4 0.8 %copy.8 = bf16[80,32,128]{2,1,0:T(8,128)(2,1)} copy(bf16[80,32,128]{2,1,0:T(8,128)(2,1)S(1)} %get-tuple-element.2) | data formatting | bytes 1310720
  36.3 0.6 %copy.9 = f32[2,80,80]{2,1,0:T(8,128)} copy(f32[2,80,80]{2,1,0:T(8,128)S(1)} %get-tuple-element.3) | data formatting | bytes 102400
Async XLA Ops:
  0.6 1.1 %copy-start = (bf16[80,32,128]{2,1,0:T(8,128)(2,1)S(1)}, bf16[80,32,128]{2,1,0:T(8,128)(2,1)}, u32[]{:S(2)}) copy-start(bf16[80,32,128]{2,1,0:T(8,128)(2,1)} %orb.1) | copy-start | bytes 1966084
  1.7 0.7 %copy-start.1 = (f32[32,128]{1,0:T(8,128)S(1)}, f32[32,128]{1,0:T(8,128)}, u32[]{:S(2)}) copy-start(f32[32,128]{1,0:T(8,128)} %pot.1) | copy-start | bytes 49156
  2.4 0.7 %copy-start.2 = (s32[2,16]{1,0:T(2,128)S(1)}, s32[2,16]{1,0:T(2,128)}, u32[]{:S(2)}) copy-start(s32[2,16]{1,0:T(2,128)} %plan.1) | copy-start | bytes 388
  3.1 0.7 %copy-start.3 = (s32[2,16]{1,0:T(2,128)S(1)}, s32[2,16]{1,0:T(2,128)}, u32[]{:S(2)}) copy-start(s32[2,16]{1,0:T(2,128)} %owners.1) | copy-start | bytes 388

commit v4 on v3

--- a/solution.py
+++ b/solution.py
@@ -12,6 +12,8 @@
 ROUNDS = 2
 CHUNK = 16
 BLOCK = 8
+VMEM_BYTES = 67043328
+SPARE_BYTES = 4096
 
 lower_edge = -2.5
 cutoff_edge = 4.0
@@ -38,10 +40,20 @@
 
 
 def body(
-    n, orb, pot, plan, owners, filt, tiles,
+    n, orb_in, pot_in, plan_in, owners_in, filt, tiles,
+    orb, pot, plan, owners, load_sem,
     wide, y0, y1, fil, matrix, send, recv, part, gathered, inverse,
     send_sem, recv_sem, relay_send, relay_recv, part_send, part_recv,
 ):
+    loads = [
+        pltpu.make_async_copy(a, b, load_sem.at[k])
+        for k, (a, b) in enumerate(
+            ((plan_in, plan), (owners_in, owners), (orb_in, orb), (pot_in, pot))
+        )
+    ]
+    for load in loads:
+        load.start()
+
     me = lax.axis_index("band")
     core = lax.rem(me, 2)
     chip = me // 2
@@ -59,6 +71,8 @@
         return c
 
     lax.fori_loop(1, n, greet, 0)
+    for load in loads:
+        load.wait()
 
     def walk(_, c):
         a, b, am, bm = c
@@ -307,20 +321,36 @@
     ).wait_send()
 
 
+def write_out(filt, tiles, filt_out, tiles_out, sem):
+    copies = [
+        pltpu.make_async_copy(filt, filt_out, sem.at[0]),
+        pltpu.make_async_copy(tiles, tiles_out, sem.at[1]),
+    ]
+    for copy in copies:
+        copy.start()
+    for copy in copies:
+        copy.wait()
+
+
 def on_device(orbitals, potential, plan, owners):
     n = lax.axis_size("band")
     bands, nx, cells = orbitals.shape
     planes = nx // n
     vmem = pl.BlockSpec(memory_space=pltpu.VMEM)
-    smem = pl.BlockSpec(memory_space=pltpu.SMEM)
     dma = pltpu.SemaphoreType.DMA
     shapes = [((bands, nx, cells), jnp.bfloat16), ((ROUNDS, bands, bands), jnp.float32)]
-    return tuple(pl.pallas_call(
+    held_bytes = bands * nx * cells * 2 + ROUNDS * bands * 128 * 4
+    held = pl.pallas_call(
         functools.partial(body, n),
         out_shape=[pltpu.VMEM(shape, dtype) for shape, dtype in shapes],
-        in_specs=[vmem, vmem, smem, smem],
+        in_specs=[pl.BlockSpec(memory_space=pltpu.HBM)] * 4,
         out_specs=[vmem, vmem],
         scratch_shapes=[
+            pltpu.VMEM((bands, nx, cells), jnp.bfloat16),
+            pltpu.VMEM((nx, cells), jnp.float32),
+            pltpu.SMEM(plan.shape, jnp.int32),
+            pltpu.SMEM(owners.shape, jnp.int32),
+            dma((4,)),
             pltpu.VMEM((CHUNK * nx, 128), jnp.float32),
             pltpu.VMEM((nx + 4, CHUNK, 128), jnp.float32),
             pltpu.VMEM((nx + 4, CHUNK, 128), jnp.float32),
@@ -339,9 +369,17 @@
             dma,
         ],
         compiler_params=pltpu.CompilerParams(
-            collective_id=0, has_side_effects=True, vmem_limit_bytes=48 * 2**20
+            collective_id=0, has_side_effects=True, vmem_limit_bytes=VMEM_BYTES - held_bytes - SPARE_BYTES
         ),
-    )(orbitals, potential, plan, owners))
+    )(orbitals, potential, plan, owners)
+    return pl.pallas_call(
+        write_out,
+        out_shape=[jax.ShapeDtypeStruct(shape, dtype) for shape, dtype in shapes],
+        in_specs=[pl.BlockSpec(memory_space=pl.ANY)] * 2,
+        out_specs=[pl.BlockSpec(memory_space=pl.ANY)] * 2,
+        scratch_shapes=[dma((2,))],
+        compiler_params=pltpu.CompilerParams(vmem_limit_bytes=2**20),
+    )(*held)
 
 
 def solution(mesh):

time: 37.2 us -> 33.5 us (0.901)
  local copies, waits for them, and re-layouts: 4.63 us -> 0 us
  Pallas kernels: 31.6 us -> 32.7 us
    unnamed x10 -> x0, local copies, waits for them, and re-layouts: 4.63 us -> none
    pallas_call x0 -> x1, Pallas kernels: none -> 0.87 us  [on_device(): pl.pallas_call(write_out, out_shape=[jax.ShapeDtypeStruct(shape, dtype) f...]
where the time goes in v4:
time: 33.5 us; the launch traced here: 33.3 us
  Pallas kernels  32.7 us (98%)
  between operations  0.64 us (2%)
    pallas_call x1, Pallas kernels, on_device(): pl.pallas_call(functools.partial(body, n), out_shape=[pltpu.VMEM(shape, d...  31.8 us
    pallas_call x1, Pallas kernels, on_device(): pl.pallas_call(write_out, out_shape=[jax.ShapeDtypeStruct(shape, dtype) f...  0.87 us

profile of v4, /device:TPU:0, one launch (start us, length us, event | category | flops | bytes accessed | tf_op | source)
XLA Modules:
  0.0 33.3 jit_solution(5079842603988248623)
XLA Ops:
  0.6 31.8 %shard_map.59 = (bf16[80,32,128]{2,1,0:T(8,128)(2,1)S(1)}, f32[2,80,80]{2,1,0:T(8,128)S(1)}) custom-call(bf16[80,32,128]{2,1,0:T(8,128)(2,1)} %orb_in.1, f32[32,128]{1,0:T(8,128)} %pot_in.1, s32[2,16]{1,0:T(2,128)} %plan_in.1, s32[2,16]{1,0:T(2,128)} %owners_in.1), custom_call_target="tpu_custom_call" | custom-call | tf_op jit(solution)/shard_map/pallas_call | solution.py:343
  32.5 0.9 %shard_map.60 = (bf16[80,32,128]{2,1,0:T(8,128)(2,1)}, f32[2,80,80]{2,1,0:T(8,128)}) custom-call(bf16[80,32,128]{2,1,0:T(8,128)(2,1)S(1)} %get-tuple-element.4.filt, f32[2,80,80]{2,1,0:T(8,128)S(1)} %get-tuple-element.5.tiles), custom_call_target="tpu_custom_call" | custom-call | tf_op jit(solution)/shard_map/pallas_call | solution.py:375
